TPU v7x, 256 devices: a whole 4x4x8 slice. The times are simulated.
256 devices in a mesh: spec: 4 (over x), geo: 64 (over y, z, core).
Axes of the slice: x: 4, y: 4, z: 8, core: 2. Of those that a mesh axis runs over, the one named last changes fastest.
Arguments:
- spectrum: bfloat16 [1296, 1024, 128], P('spec', 'geo'), may hold values from 0.01 to 11, as said below
- sea_map: int32 [1024, 128], P('geo'), may hold values 0 or 1
- depth_factor: float32 [1024, 128], P('geo'), may hold values from 0.25 to 1
- wind_speed: bfloat16 [1024, 128], P('geo'), may hold values from 0.19921875 to 2
- wind_dir: bfloat16 [1024, 128], P('geo'), may hold values from -3.140625 to 3.140625
- ice_mask: int32 [1024, 128], P('geo'), may hold values from 0 to 1, as said below
- owner_map: int32 [1024, 128], P('geo'), may hold values from 0 to 63, as said below
- pair_kernel: bfloat16 [1296, 1296], replicated, may hold values from -1 to 2
- transfer_kernel: bfloat16 [64, 1296, 1296], P('geo'), may hold values from -1 to 2
Outputs:
- updated: bfloat16 [1296, 1024, 128], P('spec', 'geo')
Inputs may be any that keep to these rules, and one draw needn't show every extreme that they name: `owner_map`: in each aligned block of 512 cells of the grid in row-major order, no owner is named by more than 16 cells, and one owner, the same in every block, is named by exactly 16 cells of each block. `ice_mask`: 1 marks ice. Cells of the owner that is named by 16 cells of every block are free of ice. `spectrum`: Positive.
All inputs are finite; a program needn't handle non-finite values. No bound on the sum of `sea_map` on one device may be relied on, other than what follows from the above.
Results may differ from a plain program's by a relative error of at most 0.0059.
Values may be sent and summed in bfloat16 or wider, within the bound.
A program may use at most 64 MiB of HBM per device.

v0:
```python
import math
import jax
import jax.numpy as jnp
from jax import lax
from jax.sharding import PartitionSpec as P

NDIR = 36


def padded_2(cells, sides, width):
    for axis, dim in sides:
        count = lax.axis_size(axis)
        ends = count - 1
        head = lax.slice_in_dim(cells, 0, width, axis=dim)
        tail = lax.slice_in_dim(cells, cells.shape[dim] - width, cells.shape[dim], axis=dim)
        cells = jnp.concatenate(
            [
                lax.ppermute(tail, axis, [(i, (i + 1) % count) for i in range(ends)]),
                cells,
                lax.ppermute(head, axis, [((i + 1) % count, i) for i in range(ends)]),
            ],
            axis=dim,
        )
    return cells


def finish(row_data, transfer, wind_rows, wind_angle):
    energy = row_data.astype(jnp.float32)
    total = jnp.mean(energy, axis=0)
    ratio = total / (1.0 + total)
    component = jnp.arange(row_data.shape[0], dtype=jnp.int32)
    heading = 2.0 * math.pi * ((component % NDIR).astype(jnp.float32) + 0.5) / NDIR
    forcing = (
        0.3
        * wind_rows.astype(jnp.float32)[None, :]
        * jnp.maximum(jnp.cos(heading[:, None] - wind_angle.astype(jnp.float32)[None, :]), 0.0)
    )
    result = (
        energy * (1.0 + forcing - 0.5 * ratio[None, :])
        + 0.2 * transfer.astype(jnp.float32) / (1.0 + total)[None, :]
    )
    return result.astype(jnp.bfloat16)


def pair_up(pair_kernel, row_data):
    coupled = jnp.dot(pair_kernel, row_data, preferred_element_type=jnp.float32)
    return (row_data.astype(jnp.float32) * coupled).astype(jnp.bfloat16)


def per_device(
    spectrum,
    sea_map,
    depth_factor,
    wind_speed,
    wind_dir,
    ice_mask,
    owner_map,
    pair_kernel,
    transfer_kernel,
):
    comp_dev, cells_x, cells_y = spectrum.shape
    spec_count = lax.axis_size("spec")
    geo_count = lax.axis_size("geo")
    rows_dev = cells_x * cells_y // spec_count
    capacity = 2 * rows_dev // geo_count
    slot_count = geo_count * capacity
    masked = spectrum * sea_map.astype(jnp.bfloat16)[None, :, :]
    padded = padded_2(masked, (("geo", 1),), 1)
    extended = padded.astype(jnp.float32)
    component = lax.axis_index("spec") * comp_dev + jnp.arange(comp_dev, dtype=jnp.int32)
    frequency = (component // NDIR).astype(jnp.float32)
    heading = 2.0 * math.pi * ((component % NDIR).astype(jnp.float32) + 0.5) / NDIR
    cosine = jnp.cos(heading)[:, None, None]
    sine = jnp.sin(heading)[:, None, None]
    gain = (jnp.float32(1.1) ** (-0.5 * frequency))[:, None, None]
    sea_weight = sea_map.astype(jnp.float32)
    step_x = 0.7 * gain * jnp.abs(cosine) * depth_factor
    step_y = 0.7 * gain * jnp.abs(sine) * depth_factor
    centre = extended[:, 1:-1]
    west_side = extended[:, :-2]
    east_side = extended[:, 2:]
    zeros_y = jnp.zeros((comp_dev, cells_x, 1), jnp.float32)
    south_side = jnp.concatenate([zeros_y, centre[:, :, :-1]], axis=2)
    north_side = jnp.concatenate([centre[:, :, 1:], zeros_y], axis=2)
    upwind_x = jnp.where(cosine > 0, west_side, east_side)
    upwind_y = jnp.where(sine > 0, south_side, north_side)
    advected = centre - step_x * (centre - upwind_x) - step_y * (centre - upwind_y)
    propagated = (advected * sea_weight).astype(jnp.bfloat16)
    flattened = propagated.reshape(comp_dev, cells_x * cells_y)
    row_data = lax.all_to_all(flattened, "spec", split_axis=1, concat_axis=0, tiled=True)
    offset = lax.axis_index("spec") * rows_dev

    def own_rows(values):
        return lax.dynamic_slice_in_dim(values.reshape(-1), offset, rows_dev)

    owners = own_rows(owner_map)
    is_live = 1 - own_rows(ice_mask)
    wind_rows = own_rows(wind_speed)
    wind_angle = own_rows(wind_dir)
    onehot = (owners[:, None] == jnp.arange(geo_count, dtype=jnp.int32)[None, :]).astype(
        jnp.int32
    ) * is_live[:, None]
    before = jnp.cumsum(onehot, axis=0) - onehot
    position = jnp.sum(before * onehot, axis=1)
    slot_index = jnp.where(is_live == 1, owners * capacity + position, slot_count)
    source = (
        jnp.full((slot_count,), rows_dev, jnp.int32)
        .at[slot_index]
        .set(jnp.arange(rows_dev, dtype=jnp.int32), mode="drop")
    )
    filled = source < rows_dev
    source_clip = jnp.minimum(source, rows_dev - 1)
    slot_clip = jnp.minimum(slot_index, slot_count - 1)

    def to_slots(values):
        return jnp.where(
            filled[None, :], jnp.take(values, source_clip, axis=1), jnp.zeros((), values.dtype)
        )

    own_kernel = transfer_kernel[0]
    outgoing = to_slots(row_data)
    wind_slots = to_slots(jnp.stack([wind_rows, wind_angle]))
    arrived, arrived_wind = (
        lax.all_to_all(outgoing, "geo", split_axis=1, concat_axis=1, tiled=True),
        lax.all_to_all(wind_slots, "geo", split_axis=1, concat_axis=1, tiled=True),
    )
    paired = pair_up(pair_kernel, arrived)
    transfer = jnp.dot(own_kernel, paired, preferred_element_type=jnp.float32).astype(jnp.bfloat16)
    sourced = finish(arrived, transfer, arrived_wind[0], arrived_wind[1])
    returned = lax.all_to_all(sourced, "geo", split_axis=1, concat_axis=1, tiled=True)
    result = jnp.where(is_live[None, :] == 1, jnp.take(returned, slot_clip, axis=1), row_data)
    restored = lax.all_to_all(result, "spec", split_axis=0, concat_axis=1, tiled=True)
    return restored.reshape(comp_dev, cells_x, cells_y)


def solution(mesh):
    placed = (
        P("spec", "geo", None),
        P("geo", None),
        P("geo", None),
        P("geo", None),
        P("geo", None),
        P("geo", None),
        P("geo", None),
        P(),
        P("geo", None, None),
    )
    return jax.shard_map(
        per_device, mesh=mesh, in_specs=placed, out_specs=P("spec", "geo", None), check_vma=False
    )
```

profile of v0, /device:TPU:1, one launch (start us, length us, event | category | flops | bytes accessed | tf_op | source)
XLA Modules:
  0.0 282.3 jit_solution(1585791736908418850)
XLA Ops:
  0.0 0.8 fusion.36
  0.8 1.7 copy_multiply_fusion
  2.5 5.1 %collective-permute-start.1 = (bf16[324,1,128]{2,0,1:T(8,128)(2,1)S(1)}, bf16[324,1,128]{2,0,1:T(8,128)(2,1)S(1)}, u32[]{:S(2)}, u32[]{:S(2)}) collective-permute-start(bf16[324,1,128]{2,0,1:T(8,128)(2,1)S(1)} %get-tuple-element.13), channel_id=1, source_target_pairs={{1,0},{2,1},{3,2},{4,3},{5,4},{6,5},{7,6},{8,7},{9,8},{10,9},{11,1... | collective-permute-start | bytes 248840 | tf_op jit(solution)/shard_map/ppermute | solution.py:20
  7.6 1.9 collective-permute-start
  9.6 0.0 copy-done.5
  9.6 0.1 dynamic-slice_subtract_fusion
  9.6 0.1 fusion.40
  9.7 0.0 copy-done.4
  9.7 0.1 dynamic_slice.13
  9.8 0.1 dynamic-slice_bitcast_fusion
  9.9 0.1 abs_multiply_fusion
  10.0 1.2 reduce-window.6
  11.2 0.2 slice_reduce_fusion
  11.4 0.1 fusion.10
  11.6 0.1 compare_and_fusion.1
  11.6 0.1 broadcast_compare_fusion.1
  11.7 0.0 collective-permute-done.1
  11.7 0.0 collective-permute-done
  11.7 0.2 maximum_convert_fusion
  12.0 0.0 copy-start.3
  12.0 0.9 fusion.34
  12.9 1.9 fusion.9
  14.8 0.2 copy.34
  15.0 0.5 all_to_all.42
  15.5 1.3 copy.35
  16.9 3.8 %all-to-all-start = ((bf16[324,4,512]{2,0,1:T(8,128)(2,1)}), bf16[324,4,512]{2,0,1:T(8,128)(2,1)S(1)}, u32[]{:S(2)}, u32[]{:S(2)}) async-start(bf16[324,4,512]{2,0,1:T(8,128)(2,1)} %copy.35), calls=%async_computation | async-start | bytes 2686976 | tf_op jit(solution)/shard_map/all_to_all | solution.py:90
  20.7 0.1 compare_select_fusion.1
  20.7 2.4 scatter_custom_fusion
  23.2 0.1 broadcast_in_dim.115
  23.3 0.1 broadcast_in_dim.113
  23.4 0.8 dynamic_slice.15
  24.1 0.8 dynamic_slice.14
  24.9 0.2 copy.38
  25.1 3.2 %gather_fusion.1 = bf16[1024,2]{1,0:T(8,128)(2,1)S(1)} fusion(bf16[2,512]{0,1:T(8,128)(2,1)S(1)} %copy.38, s32[1024]{0:T(1024)S(1)} %fusion.21), kind=kCustom, calls=%fused_computation.1 | custom fusion | bytes 12288 | tf_op jit(solution)/shard_map/jit(_take)/gather | solution.py:117
  28.3 0.5 copy.39
  28.8 0.7 broadcast_select_fusion.1
  29.5 9.3 %all-to-all-done = bf16[324,4,512]{2,0,1:T(8,128)(2,1)S(1)} async-done(((bf16[324,4,512]{2,0,1:T(8,128)(2,1)}), bf16[324,4,512]{2,0,1:T(8,128)(2,1)S(1)}, u32[]{:S(2)}, u32[]{:S(2)}) %all-to-all-start) | async-done | bytes 1327136 | tf_op jit(solution)/shard_map/all_to_all | solution.py:90
  38.8 12.4 %all-to-all-start.2 = ((bf16[2,64,16]{2,0,1:T(2,128)(2,1)}), bf16[2,64,16]{2,0,1:T(2,128)(2,1)S(1)}, u32[]{:S(2)}, u32[]{:S(2)}) async-start(bf16[2,64,16]{2,0,1:T(2,128)(2,1)} %broadcast_select_fusion.1), calls=%async_computation.2 | async-start | bytes 65536 | tf_op jit(solution)/shard_map/all_to_all | solution.py:125
  51.2 0.3 all_to_all.45
  51.5 0.8 copy.36
  52.4 5.5 %gather_fusion = bf16[1024,1296]{1,0:T(8,128)(2,1)} fusion(bf16[1296,512]{0,1:T(8,128)(2,1)S(1)} %copy.36, s32[1024]{0:T(1024)S(1)} %fusion.21), kind=kCustom, calls=%fused_computation | custom fusion | bytes 5312512 | tf_op jit(solution)/shard_map/jit(_take)/gather | solution.py:117
  57.9 3.3 %select_select_fusion = bf16[1296,64,16]{0,2,1:T(8,128)(2,1)} fusion(bf16[1296,64,16]{0,2,1:T(8,128)(2,1)} %bitcast.76, pred[64,16]{1,0:T(8,128)(4,1)S(1)} %broadcast_in_dim.115, pred[64,16]{1,0:T(8,128)(4,1)S(1)} %broadcast_in_dim.113), kind=kLoop, calls=%fused_computation.12 | loop fusion | flops 2654208 | bytes 5310464 | tf_op jit(solution)/shard_map/jit(_where)/select_n | solution.py:116
  61.2 0.0 all-to-all-done.2
  61.2 10.3 %all-to-all-start.1 = ((bf16[1296,64,16]{0,2,1:T(8,128)(2,1)}), bf16[1296,64,16]{0,2,1:T(8,128)(2,1)S(1)}, u32[]{:S(2)}, u32[]{:S(2)}) async-start(bf16[1296,64,16]{0,2,1:T(8,128)(2,1)} %select_select_fusion), calls=%async_computation.1 | async-start | bytes 5767168 | tf_op jit(solution)/shard_map/all_to_all | solution.py:124
  71.6 0.2 fusion.14
  71.8 0.1 reshape.197
  71.8 0.1 mul.195
  71.9 67.5 %all-to-all-done.1 = bf16[1296,64,16]{0,2,1:T(8,128)(2,1)S(1)} async-done(((bf16[1296,64,16]{0,2,1:T(8,128)(2,1)}), bf16[1296,64,16]{0,2,1:T(8,128)(2,1)S(1)}, u32[]{:S(2)}, u32[]{:S(2)}) %all-to-all-start.1) | async-done | bytes 2654240 | tf_op jit(solution)/shard_map/all_to_all | solution.py:124
  139.4 2.8 copy.37
  142.2 0.5 convert_reduce_fusion
  142.6 0.1 div.58
  142.7 0.0 copy-start.6
  142.8 7.1 %fusion.58 = bf16[1296,1024]{1,0:T(8,128)(2,1)S(1)} fusion(bf16[1296,1296]{1,0:T(8,128)(2,1)} %param.16, bf16[1296,1024]{0,1:T(8,128)(2,1)S(1)} %bitcast.73, bf16[1296,1024]{1,0:T(8,128)(2,1)} %copy.37), kind=kOutput, calls=%bitcast_fusion.1.clone.1 | convolution fusion | flops 3443834880 | bytes 11321856 | tf_op jit(solution)/shard_map/dot_general | solution.py:46
  149.9 22.4 %fusion.1 = bf16[1296,1024]{1,0:T(8,128)(2,1)S(1)} fusion(bf16[1296,1024]{1,0:T(8,128)(2,1)S(1)} %copy-done.2, bf16[1,1296,1296]{2,1,0:T(8,128)(2,1)S(1)} %copy-done.6, f32[1024]{0:T(1024)S(1)} %get-tuple-element.17, f32[1024]{0:T(1024)S(1)} %get-tuple-element.16, f32[1024]{0:T(1024)S(1)} %reshape.197, f32[1296]{0:T(1024)S(1)} %fusion.17, ...), kind=kOutput, calls=%fused_computation.8 | convolution fusion | flops 3457105920 | bytes 11343424 | tf_op jit(solution)/shard_map/dot_general | solution.py:128
  172.3 2.9 %copy.40 = bf16[1296,1024]{0,1:T(8,128)(2,1)} copy(bf16[1296,1024]{1,0:T(8,128)(2,1)S(1)} %fusion.1) | data formatting | bytes 5308416 | tf_op jit(solution)/shard_map/convert_element_type | solution.py:42
  175.2 5.7 %all-to-all-start.3 = ((bf16[1296,64,16]{0,2,1:T(8,128)(2,1)}), bf16[1296,64,16]{0,2,1:T(8,128)(2,1)S(1)}, u32[]{:S(2)}, u32[]{:S(2)}) async-start(bf16[1296,64,16]{0,2,1:T(8,128)(2,1)} %bitcast.75), calls=%async_computation.3 | async-start | bytes 5767168 | tf_op jit(solution)/shard_map/all_to_all | solution.py:130
  181.0 67.9 %all-to-all-done.3 = bf16[1296,64,16]{0,2,1:T(8,128)(2,1)S(1)} async-done(((bf16[1296,64,16]{0,2,1:T(8,128)(2,1)}), bf16[1296,64,16]{0,2,1:T(8,128)(2,1)S(1)}, u32[]{:S(2)}, u32[]{:S(2)}) %all-to-all-start.3) | async-done | bytes 2654240 | tf_op jit(solution)/shard_map/all_to_all | solution.py:130
  248.8 2.9 %gather_fusion.2 = bf16[512,1296]{1,0:T(8,128)(2,1)} fusion(bf16[1296,1024]{0,1:T(8,128)(2,1)S(1)} %bitcast.71, s32[1024]{0:T(1024)S(1)} %pad_clamp_fusion), kind=kCustom, calls=%fused_computation.2 | custom fusion | bytes 2656256 | tf_op jit(solution)/shard_map/jit(_take)/gather | solution.py:131
  251.7 3.8 %reshape.234 = bf16[4,324,512]{1,0,2:T(4,128)(2,1)S(1)} reshape(bf16[1296,512]{0,1:T(8,128)(2,1)} %bitcast.78) | data formatting | bytes 2654208 | tf_op jit(solution)/shard_map/jit(_take)/gather | solution.py:131
  255.5 2.5 copy.43
  258.0 1.5 select_select_fusion.1
  259.4 20.8 %all_to_all.59 = bf16[4,324,512]{2,1,0:T(8,128)(2,1)S(1)} all-to-all(bf16[4,324,512]{2,1,0:T(8,128)(2,1)S(1)} %select_select_fusion.1), channel_id=1, replica_groups=mesh['spec'=4,'geo'=64] {'spec'}, dimensions={0} | all-to-all | bytes 2654208 | tf_op jit(solution)/shard_map/all_to_all | solution.py:132
  280.2 0.7 copy.42
  280.9 1.4 reshape.196
  (24 shorter events, 0.2 us)
Async XLA Ops:
  0.0 9.6 %copy-start.5 = (s32[16,128]{1,0:T(8,128)S(1)}, s32[16,128]{1,0:T(8,128)}, u32[]{:S(2)}) copy-start(s32[16,128]{1,0:T(8,128)} %param.14) | copy-start | bytes 24580
  0.0 9.7 %copy-start.4 = (s32[16,128]{1,0:T(8,128)S(1)}, s32[16,128]{1,0:T(8,128)}, u32[]{:S(2)}) copy-start(s32[16,128]{1,0:T(8,128)} %param.15) | copy-start | bytes 24580
  2.5 9.2 %collective-permute-start.1 = (bf16[324,1,128]{2,0,1:T(8,128)(2,1)S(1)}, bf16[324,1,128]{2,0,1:T(8,128)(2,1)S(1)}, u32[]{:S(2)}, u32[]{:S(2)}) collective-permute-start(bf16[324,1,128]{2,0,1:T(8,128)(2,1)S(1)} %get-tuple-element.13), channel_id=1, source_target_pairs={{1,0},{2,1},{3,2},{4,3},{5,4},{6,5},{7,6},{8,7},{9,8},{10,9},{11,1... | collective-permute-start | bytes 248840 | tf_op jit(solution)/shard_map/ppermute | solution.py:20
  7.6 4.1 %collective-permute-start = (bf16[324,1,128]{2,0,1:T(8,128)(2,1)S(1)}, bf16[324,1,128]{2,0,1:T(8,128)(2,1)S(1)}, u32[]{:S(2)}, u32[]{:S(2)}) collective-permute-start(bf16[324,1,128]{2,0,1:T(8,128)(2,1)S(1)} %get-tuple-element.12), channel_id=1, source_target_pairs={{0,1},{1,2},{2,3},{3,4},{4,5},{5,6},{6,7},{7,8},{8,9},{9,10},{10,1... | collective-permute-start | bytes 248840 | tf_op jit(solution)/shard_map/ppermute | solution.py:18
  12.0 0.9 copy-start.3
  16.9 22.0 %all-to-all-start = ((bf16[324,4,512]{2,0,1:T(8,128)(2,1)}), bf16[324,4,512]{2,0,1:T(8,128)(2,1)S(1)}, u32[]{:S(2)}, u32[]{:S(2)}) async-start(bf16[324,4,512]{2,0,1:T(8,128)(2,1)} %copy.35), calls=%async_computation | async-start | bytes 2686976 | tf_op jit(solution)/shard_map/all_to_all | solution.py:90
  38.8 12.4 %copy-start = (bf16[324,4,512]{2,0,1:T(8,128)(2,1)}, bf16[324,4,512]{2,0,1:T(8,128)(2,1)S(1)}, u32[]{:S(2)}) copy-start(bf16[324,4,512]{2,0,1:T(8,128)(2,1)S(1)} %all-to-all-done) | copy-start | bytes 3981316
  38.8 22.4 %all-to-all-start.2 = ((bf16[2,64,16]{2,0,1:T(2,128)(2,1)}), bf16[2,64,16]{2,0,1:T(2,128)(2,1)S(1)}, u32[]{:S(2)}, u32[]{:S(2)}) async-start(bf16[2,64,16]{2,0,1:T(2,128)(2,1)} %broadcast_select_fusion.1), calls=%async_computation.2 | async-start | bytes 65536 | tf_op jit(solution)/shard_map/all_to_all | solution.py:125
  61.2 78.2 %all-to-all-start.1 = ((bf16[1296,64,16]{0,2,1:T(8,128)(2,1)}), bf16[1296,64,16]{0,2,1:T(8,128)(2,1)S(1)}, u32[]{:S(2)}, u32[]{:S(2)}) async-start(bf16[1296,64,16]{0,2,1:T(8,128)(2,1)} %select_select_fusion), calls=%async_computation.1 | async-start | bytes 5767168 | tf_op jit(solution)/shard_map/all_to_all | solution.py:124
  142.7 7.2 %copy-start.2 = (bf16[1296,1024]{1,0:T(8,128)(2,1)S(1)}, bf16[1296,1024]{1,0:T(8,128)(2,1)}, u32[]{:S(2)}) copy-start(bf16[1296,1024]{1,0:T(8,128)(2,1)} %copy.37) | copy-start | bytes 7962628
  142.7 7.2 %copy-start.6 = (bf16[1,1296,1296]{2,1,0:T(8,128)(2,1)S(1)}, bf16[1,1296,1296]{2,1,0:T(8,128)(2,1)}, u32[]{:S(2)}) copy-start(bf16[1,1296,1296]{2,1,0:T(8,128)(2,1)} %param.17) | copy-start | bytes 10077700
  175.2 73.6 %all-to-all-start.3 = ((bf16[1296,64,16]{0,2,1:T(8,128)(2,1)}), bf16[1296,64,16]{0,2,1:T(8,128)(2,1)S(1)}, u32[]{:S(2)}, u32[]{:S(2)}) async-start(bf16[1296,64,16]{0,2,1:T(8,128)(2,1)} %bitcast.75), calls=%async_computation.3 | async-start | bytes 5767168 | tf_op jit(solution)/shard_map/all_to_all | solution.py:130
  251.7 6.2 %copy-start.1 = (bf16[324,4,512]{2,0,1:T(8,128)(2,1)S(1)}, bf16[324,4,512]{2,0,1:T(8,128)(2,1)}, u32[]{:S(2)}) copy-start(bf16[324,4,512]{2,0,1:T(8,128)(2,1)} %copy-done) | copy-start | bytes 3981316
where the time goes:
time: 283 us; the launch traced here: 282 us
  waiting for transfers between devices  145 us (51%)
  starting transfers between devices  39.3 us (14%)
  local copies, waits for them, and re-layouts  35 us (12%)
  matrix products  29.5 us (10%)
  blocking collectives  20.8 us (7%)
  other arithmetic  12.6 us (4%)
    all_to_all x1, waiting for transfers between devices, per_device(): lax.all_to_all(sourced, 'geo', split_axis=1, concat_axis=1, tiled=True)  67.9 us
    all_to_all x1, waiting for transfers between devices, per_device(): lax.all_to_all(outgoing, 'geo', split_axis=1, concat_axis=1, tiled=True)  67.5 us
    dot_general x1, matrix products, per_device(): jnp.dot(own_kernel, paired, preferred_element_type=jnp.float32)  22.4 us
    all_to_all x1, blocking collectives, per_device(): lax.all_to_all(result, 'spec', split_axis=0, concat_axis=1, tiled=True)  20.8 us
    all_to_all x1, starting transfers between devices, per_device(): lax.all_to_all(wind_slots, 'geo', split_axis=1, concat_axis=1, tiled=True)  12.4 us
    all_to_all x1, starting transfers between devices, per_device(): lax.all_to_all(outgoing, 'geo', split_axis=1, concat_axis=1, tiled=True)  10.3 us
    all_to_all x1, waiting for transfers between devices, per_device(): lax.all_to_all(flattened, 'spec', split_axis=1, concat_axis=0, tiled=True)  9.32 us
    gather x3, local copies, waits for them, and re-layouts, to_slots(): jnp.take(values, source_clip, axis=1)  9.2 us
  transfers between devices with their start and end apart: 6, of which 3 were waited for; matrix products, arithmetic and copies ran while one was open for 7% of the time, Pallas kernels for 0%

commit v1 on v0

--- a/solution.py
+++ b/solution.py
@@ -5,6 +5,28 @@
 from jax.sharding import PartitionSpec as P
 
 NDIR = 36
+
+
+def in_blocks(shard, dim, size):
+    before, after = (shard.shape[:dim], shard.shape[dim + 1 :])
+    return jnp.moveaxis(shard.reshape(*before, size, -1, *after), dim, 0)
+
+
+def in_order(parts, dim):
+    lengths = list(parts.shape[1:])
+    lengths[dim] *= parts.shape[0]
+    return jnp.moveaxis(parts, 0, dim).reshape(lengths)
+
+
+def swapped_with_each(array, axis, split_dim, concat_dim):
+    length, position = (lax.axis_size(axis), lax.axis_index(axis))
+    parts = in_blocks(array, split_dim, length)
+    done = [parts[position]]
+    for lap in range(1, length):
+        sent = parts[position ^ lap]
+        done.append(lax.ppermute(sent, axis, [(i, i ^ lap) for i in range(length)]))
+    parts = jnp.stack(done)[position ^ jnp.arange(length)]
+    return in_order(parts, concat_dim)
 
 
 def padded_2(cells, sides, width):
@@ -129,7 +151,7 @@
     sourced = finish(arrived, transfer, arrived_wind[0], arrived_wind[1])
     returned = lax.all_to_all(sourced, "geo", split_axis=1, concat_axis=1, tiled=True)
     result = jnp.where(is_live[None, :] == 1, jnp.take(returned, slot_clip, axis=1), row_data)
-    restored = lax.all_to_all(result, "spec", split_axis=0, concat_axis=1, tiled=True)
+    restored = swapped_with_each(result, "spec", 0, 1)
     return restored.reshape(comp_dev, cells_x, cells_y)
 
 

time: 283 us -> 281 us (level)
  blocking collectives: 20.8 us -> 0 us
  waiting for transfers between devices: 145 us -> 160 us
  starting transfers between devices: 39.3 us -> 42.6 us
    all_to_all x1 -> x0, blocking collectives: 20.8 us -> none  [per_device(): lax.all_to_all(result, 'spec', split_axis=0, concat_axis=1, tiled=True)]
    ppermute x0 -> x3, waiting for transfers between devices: none -> 14.9 us  [swapped_with_each(): done.append(lax.ppermute(sent, axis, [(i, i ^ lap) for i in range(length)]))]
    ppermute x0 -> x3, starting transfers between devices: none -> 3.34 us  [swapped_with_each(): done.append(lax.ppermute(sent, axis, [(i, i ^ lap) for i in range(length)]))]
  transfers between devices with their start and end apart: 6 -> 9, of which waited for: 3 -> 5; matrix products, arithmetic and copies ran while one was open for 7% -> 7% of each run, Pallas kernels for 0% -> 0%
where the time goes in v1:
time: 281 us
  waiting for transfers between devices  160 us (57%)
  starting transfers between devices  42.6 us (15%)
  local copies, waits for them, and re-layouts  35.8 us (13%)
  matrix products  29.5 us (10%)
  other arithmetic  12.8 us (5%)
    all_to_all x1, waiting for transfers between devices, per_device(): lax.all_to_all(sourced, 'geo', split_axis=1, concat_axis=1, tiled=True)  67.8 us
    all_to_all x1, waiting for transfers between devices, per_device(): lax.all_to_all(outgoing, 'geo', split_axis=1, concat_axis=1, tiled=True)  67.5 us
    dot_general x1, matrix products, per_device(): jnp.dot(own_kernel, paired, preferred_element_type=jnp.float32)  22.4 us
    ppermute x3, waiting for transfers between devices, swapped_with_each(): done.append(lax.ppermute(sent, axis, [(i, i ^ lap) for i in range(length)]))  14.9 us
    all_to_all x1, starting transfers between devices, per_device(): lax.all_to_all(wind_slots, 'geo', split_axis=1, concat_axis=1, tiled=True)  12.4 us
    all_to_all x1, starting transfers between devices, per_device(): lax.all_to_all(outgoing, 'geo', split_axis=1, concat_axis=1, tiled=True)  10.3 us
    all_to_all x1, waiting for transfers between devices, per_device(): lax.all_to_all(flattened, 'spec', split_axis=1, concat_axis=0, tiled=True)  9.32 us
    gather x3, local copies, waits for them, and re-layouts, to_slots(): jnp.take(values, source_clip, axis=1)  9.22 us
  transfers between devices with their start and end apart: 9, of which 5 were waited for; matrix products, arithmetic and copies ran while one was open for 7% of the time, Pallas kernels for 0%

profile of v1, /device:TPU:1, one launch (start us, length us, event | category | flops | bytes accessed | tf_op | source)
XLA Modules:
  0.0 280.7 jit_solution(13859204161156552275)
XLA Ops:
  0.0 0.8 fusion.37
  0.8 1.7 copy_multiply_fusion
  2.5 5.1 %collective-permute-start.1 = (bf16[324,1,128]{2,0,1:T(8,128)(2,1)S(1)}, bf16[324,1,128]{2,0,1:T(8,128)(2,1)S(1)}, u32[]{:S(2)}, u32[]{:S(2)}) collective-permute-start(bf16[324,1,128]{2,0,1:T(8,128)(2,1)S(1)} %get-tuple-element.17), channel_id=1, source_target_pairs={{1,0},{2,1},{3,2},{4,3},{5,4},{6,5},{7,6},{8,7},{9,8},{10,9},{11,1... | collective-permute-start | bytes 248840 | tf_op jit(solution)/shard_map/ppermute | solution.py:42
  7.6 1.9 collective-permute-start
  9.6 0.1 dynamic-slice_subtract_fusion
  9.6 0.1 fusion.41
  9.7 0.1 dynamic_slice.25
  9.8 0.1 dynamic-slice_bitcast_fusion.3
  9.9 0.1 abs_multiply_fusion
  10.0 1.2 reduce-window.6
  11.2 0.2 slice_reduce_fusion
  11.4 0.1 fusion.10
  11.6 0.1 compare_and_fusion.1
  11.6 0.1 broadcast_compare_fusion.1
  11.7 0.2 maximum_convert_fusion
  12.0 0.9 fusion.35
  12.9 1.9 fusion.9
  14.8 0.2 copy.34
  15.0 0.5 all_to_all.32
  15.5 1.3 copy.35
  16.9 3.8 %all-to-all-start = ((bf16[324,4,512]{2,0,1:T(8,128)(2,1)}), bf16[324,4,512]{2,0,1:T(8,128)(2,1)S(1)}, u32[]{:S(2)}, u32[]{:S(2)}) async-start(bf16[324,4,512]{2,0,1:T(8,128)(2,1)} %copy.35), calls=%async_computation | async-start | bytes 2686976 | tf_op jit(solution)/shard_map/all_to_all | solution.py:112
  20.7 0.1 compare_select_fusion.1
  20.8 2.4 scatter_custom_fusion
  23.2 0.1 broadcast_in_dim.116
  23.3 0.1 broadcast_in_dim.114
  23.4 0.8 dynamic_slice.27
  24.2 0.8 dynamic_slice.26
  24.9 0.2 copy.38
  25.1 3.2 %gather_fusion.1 = bf16[1024,2]{1,0:T(8,128)(2,1)S(1)} fusion(bf16[2,512]{0,1:T(8,128)(2,1)S(1)} %copy.38, s32[1024]{0:T(1024)S(1)} %fusion.21), kind=kCustom, calls=%fused_computation.1 | custom fusion | bytes 12288 | tf_op jit(solution)/shard_map/jit(_take)/gather | solution.py:139
  28.4 0.5 copy.39
  28.8 0.7 broadcast_select_fusion.1
  29.5 9.3 %all-to-all-done = bf16[324,4,512]{2,0,1:T(8,128)(2,1)S(1)} async-done(((bf16[324,4,512]{2,0,1:T(8,128)(2,1)}), bf16[324,4,512]{2,0,1:T(8,128)(2,1)S(1)}, u32[]{:S(2)}, u32[]{:S(2)}) %all-to-all-start) | async-done | bytes 1327136 | tf_op jit(solution)/shard_map/all_to_all | solution.py:112
  38.9 12.4 %all-to-all-start.2 = ((bf16[2,64,16]{2,0,1:T(2,128)(2,1)}), bf16[2,64,16]{2,0,1:T(2,128)(2,1)S(1)}, u32[]{:S(2)}, u32[]{:S(2)}) async-start(bf16[2,64,16]{2,0,1:T(2,128)(2,1)} %broadcast_select_fusion.1), calls=%async_computation.2 | async-start | bytes 65536 | tf_op jit(solution)/shard_map/all_to_all | solution.py:147
  51.2 0.3 all_to_all.35
  51.6 0.8 copy.36
  52.4 5.5 %gather_fusion = bf16[1024,1296]{1,0:T(8,128)(2,1)} fusion(bf16[1296,512]{0,1:T(8,128)(2,1)S(1)} %copy.36, s32[1024]{0:T(1024)S(1)} %fusion.21), kind=kCustom, calls=%fused_computation | custom fusion | bytes 5312512 | tf_op jit(solution)/shard_map/jit(_take)/gather | solution.py:139
  57.9 3.3 %select_select_fusion = bf16[1296,64,16]{0,2,1:T(8,128)(2,1)} fusion(bf16[1296,64,16]{0,2,1:T(8,128)(2,1)} %bitcast.87, pred[64,16]{1,0:T(8,128)(4,1)S(1)} %broadcast_in_dim.116, pred[64,16]{1,0:T(8,128)(4,1)S(1)} %broadcast_in_dim.114), kind=kLoop, calls=%fused_computation.13 | loop fusion | flops 2654208 | bytes 5310464 | tf_op jit(solution)/shard_map/jit(_where)/select_n | solution.py:138
  61.2 10.3 %all-to-all-start.1 = ((bf16[1296,64,16]{0,2,1:T(8,128)(2,1)}), bf16[1296,64,16]{0,2,1:T(8,128)(2,1)S(1)}, u32[]{:S(2)}, u32[]{:S(2)}) async-start(bf16[1296,64,16]{0,2,1:T(8,128)(2,1)} %select_select_fusion), calls=%async_computation.1 | async-start | bytes 5767168 | tf_op jit(solution)/shard_map/all_to_all | solution.py:146
  71.6 0.2 fusion.14
  71.8 0.1 reshape.206
  71.8 0.1 mul.195
  71.9 67.5 %all-to-all-done.1 = bf16[1296,64,16]{0,2,1:T(8,128)(2,1)S(1)} async-done(((bf16[1296,64,16]{0,2,1:T(8,128)(2,1)}), bf16[1296,64,16]{0,2,1:T(8,128)(2,1)S(1)}, u32[]{:S(2)}, u32[]{:S(2)}) %all-to-all-start.1) | async-done | bytes 2654240 | tf_op jit(solution)/shard_map/all_to_all | solution.py:146
  139.4 2.8 copy.37
  142.2 0.5 convert_reduce_fusion
  142.6 0.1 div.58
  142.8 7.1 %fusion.59 = bf16[1296,1024]{1,0:T(8,128)(2,1)S(1)} fusion(bf16[1296,1296]{1,0:T(8,128)(2,1)} %param.16, bf16[1296,1024]{0,1:T(8,128)(2,1)S(1)} %bitcast.84, bf16[1296,1024]{1,0:T(8,128)(2,1)} %copy.37), kind=kOutput, calls=%bitcast_fusion.1.clone.1 | convolution fusion | flops 3443834880 | bytes 11321856 | tf_op jit(solution)/shard_map/dot_general | solution.py:68
  149.9 22.4 %fusion.1 = bf16[1296,1024]{1,0:T(8,128)(2,1)S(1)} fusion(bf16[1296,1024]{1,0:T(8,128)(2,1)S(1)} %copy-done.2, bf16[1,1296,1296]{2,1,0:T(8,128)(2,1)S(1)} %copy-done.6, f32[1024]{0:T(1024)S(1)} %get-tuple-element.21, f32[1024]{0:T(1024)S(1)} %get-tuple-element.20, f32[1024]{0:T(1024)S(1)} %reshape.206, f32[1296]{0:T(1024)S(1)} %fusion.17, ...), kind=kOutput, calls=%fused_computation.9 | convolution fusion | flops 3457105920 | bytes 11343424 | tf_op jit(solution)/shard_map/dot_general | solution.py:150
  172.3 2.8 %copy.40 = bf16[1296,1024]{0,1:T(8,128)(2,1)} copy(bf16[1296,1024]{1,0:T(8,128)(2,1)S(1)} %fusion.1) | data formatting | bytes 5308416 | tf_op jit(solution)/shard_map/convert_element_type | solution.py:64
  175.2 5.7 %all-to-all-start.3 = ((bf16[1296,64,16]{0,2,1:T(8,128)(2,1)}), bf16[1296,64,16]{0,2,1:T(8,128)(2,1)S(1)}, u32[]{:S(2)}, u32[]{:S(2)}) async-start(bf16[1296,64,16]{0,2,1:T(8,128)(2,1)} %bitcast.86), calls=%async_computation.3 | async-start | bytes 5767168 | tf_op jit(solution)/shard_map/all_to_all | solution.py:152
  181.0 67.8 %all-to-all-done.3 = bf16[1296,64,16]{0,2,1:T(8,128)(2,1)S(1)} async-done(((bf16[1296,64,16]{0,2,1:T(8,128)(2,1)}), bf16[1296,64,16]{0,2,1:T(8,128)(2,1)S(1)}, u32[]{:S(2)}, u32[]{:S(2)}) %all-to-all-start.3) | async-done | bytes 2654240 | tf_op jit(solution)/shard_map/all_to_all | solution.py:152
  248.8 2.9 %gather_fusion.2 = bf16[512,1296]{1,0:T(8,128)(2,1)} fusion(bf16[1296,1024]{0,1:T(8,128)(2,1)S(1)} %bitcast.82, s32[1024]{0:T(1024)S(1)} %pad_clamp_fusion.1), kind=kCustom, calls=%fused_computation.2 | custom fusion | bytes 2656256 | tf_op jit(solution)/shard_map/jit(_take)/gather | solution.py:153
  251.7 3.8 %reshape.251 = bf16[4,324,512]{1,0,2:T(4,128)(2,1)S(1)} reshape(bf16[1296,512]{0,1:T(8,128)(2,1)} %bitcast.89) | data formatting | bytes 2654208 | tf_op jit(solution)/shard_map/jit(_take)/gather | solution.py:153
  255.5 2.5 copy.43
  258.0 1.5 select_select_fusion.1
  259.5 0.1 constant_dynamic-slice_fusion
  259.6 1.0 collective-permute-start.4
  260.6 1.2 collective-permute-start.3
  261.7 1.2 collective-permute-start.2
  262.9 14.6 %collective-permute-done.4 = bf16[324,512]{1,0:T(8,128)(2,1)S(1)} collective-permute-done((bf16[324,512]{1,0:T(8,128)(2,1)S(1)}, bf16[324,512]{1,0:T(8,128)(2,1)S(1)}, u32[]{:S(2)}, u32[]{:S(2)}) %collective-permute-start.4) | collective-permute-done | bytes 331808 | tf_op jit(solution)/shard_map/ppermute | solution.py:27
  277.5 0.3 collective-permute-done.2
  277.8 0.2 pad_maximum_fusion
  278.0 0.6 gather_fusion.3
  278.6 0.7 copy.42
  279.3 1.4 reshape_reshape.3
  (34 shorter events, 0.2 us)
Async XLA Ops:
  0.0 9.6 %copy-start.5 = (s32[16,128]{1,0:T(8,128)S(1)}, s32[16,128]{1,0:T(8,128)}, u32[]{:S(2)}) copy-start(s32[16,128]{1,0:T(8,128)} %param.14) | copy-start | bytes 24580
  0.0 9.7 %copy-start.4 = (s32[16,128]{1,0:T(8,128)S(1)}, s32[16,128]{1,0:T(8,128)}, u32[]{:S(2)}) copy-start(s32[16,128]{1,0:T(8,128)} %param.15) | copy-start | bytes 24580
  2.5 9.2 %collective-permute-start.1 = (bf16[324,1,128]{2,0,1:T(8,128)(2,1)S(1)}, bf16[324,1,128]{2,0,1:T(8,128)(2,1)S(1)}, u32[]{:S(2)}, u32[]{:S(2)}) collective-permute-start(bf16[324,1,128]{2,0,1:T(8,128)(2,1)S(1)} %get-tuple-element.17), channel_id=1, source_target_pairs={{1,0},{2,1},{3,2},{4,3},{5,4},{6,5},{7,6},{8,7},{9,8},{10,9},{11,1... | collective-permute-start | bytes 248840 | tf_op jit(solution)/shard_map/ppermute | solution.py:42
  7.6 4.1 %collective-permute-start = (bf16[324,1,128]{2,0,1:T(8,128)(2,1)S(1)}, bf16[324,1,128]{2,0,1:T(8,128)(2,1)S(1)}, u32[]{:S(2)}, u32[]{:S(2)}) collective-permute-start(bf16[324,1,128]{2,0,1:T(8,128)(2,1)S(1)} %get-tuple-element.16), channel_id=1, source_target_pairs={{0,1},{1,2},{2,3},{3,4},{4,5},{5,6},{6,7},{7,8},{8,9},{9,10},{10,1... | collective-permute-start | bytes 248840 | tf_op jit(solution)/shard_map/ppermute | solution.py:40
  12.0 0.9 copy-start.3
  16.9 22.0 %all-to-all-start = ((bf16[324,4,512]{2,0,1:T(8,128)(2,1)}), bf16[324,4,512]{2,0,1:T(8,128)(2,1)S(1)}, u32[]{:S(2)}, u32[]{:S(2)}) async-start(bf16[324,4,512]{2,0,1:T(8,128)(2,1)} %copy.35), calls=%async_computation | async-start | bytes 2686976 | tf_op jit(solution)/shard_map/all_to_all | solution.py:112
  38.9 12.4 %copy-start = (bf16[324,4,512]{2,0,1:T(8,128)(2,1)}, bf16[324,4,512]{2,0,1:T(8,128)(2,1)S(1)}, u32[]{:S(2)}) copy-start(bf16[324,4,512]{2,0,1:T(8,128)(2,1)S(1)} %all-to-all-done) | copy-start | bytes 3981316
  38.9 22.4 %all-to-all-start.2 = ((bf16[2,64,16]{2,0,1:T(2,128)(2,1)}), bf16[2,64,16]{2,0,1:T(2,128)(2,1)S(1)}, u32[]{:S(2)}, u32[]{:S(2)}) async-start(bf16[2,64,16]{2,0,1:T(2,128)(2,1)} %broadcast_select_fusion.1), calls=%async_computation.2 | async-start | bytes 65536 | tf_op jit(solution)/shard_map/all_to_all | solution.py:147
  61.2 78.2 %all-to-all-start.1 = ((bf16[1296,64,16]{0,2,1:T(8,128)(2,1)}), bf16[1296,64,16]{0,2,1:T(8,128)(2,1)S(1)}, u32[]{:S(2)}, u32[]{:S(2)}) async-start(bf16[1296,64,16]{0,2,1:T(8,128)(2,1)} %select_select_fusion), calls=%async_computation.1 | async-start | bytes 5767168 | tf_op jit(solution)/shard_map/all_to_all | solution.py:146
  142.7 7.2 %copy-start.2 = (bf16[1296,1024]{1,0:T(8,128)(2,1)S(1)}, bf16[1296,1024]{1,0:T(8,128)(2,1)}, u32[]{:S(2)}) copy-start(bf16[1296,1024]{1,0:T(8,128)(2,1)} %copy.37) | copy-start | bytes 7962628
  142.7 7.2 %copy-start.6 = (bf16[1,1296,1296]{2,1,0:T(8,128)(2,1)S(1)}, bf16[1,1296,1296]{2,1,0:T(8,128)(2,1)}, u32[]{:S(2)}) copy-start(bf16[1,1296,1296]{2,1,0:T(8,128)(2,1)} %param.17) | copy-start | bytes 10077700
  175.2 73.6 %all-to-all-start.3 = ((bf16[1296,64,16]{0,2,1:T(8,128)(2,1)}), bf16[1296,64,16]{0,2,1:T(8,128)(2,1)S(1)}, u32[]{:S(2)}, u32[]{:S(2)}) async-start(bf16[1296,64,16]{0,2,1:T(8,128)(2,1)} %bitcast.86), calls=%async_computation.3 | async-start | bytes 5767168 | tf_op jit(solution)/shard_map/all_to_all | solution.py:152
  251.7 6.3 %copy-start.1 = (bf16[324,4,512]{2,0,1:T(8,128)(2,1)S(1)}, bf16[324,4,512]{2,0,1:T(8,128)(2,1)}, u32[]{:S(2)}) copy-start(bf16[324,4,512]{2,0,1:T(8,128)(2,1)} %copy-done) | copy-start | bytes 3981316
  259.6 17.9 %collective-permute-start.4 = (bf16[324,512]{1,0:T(8,128)(2,1)S(1)}, bf16[324,512]{1,0:T(8,128)(2,1)S(1)}, u32[]{:S(2)}, u32[]{:S(2)}) collective-permute-start(bf16[324,512]{1,0:T(8,128)(2,1)S(1)} %get-tuple-element.13), channel_id=1, source_target_pairs={{0,192},{64,128},{128,64},{192,0},{1,193},{65,129},{129,65},{193,1... | collective-permute-start | bytes 995336 | tf_op jit(solution)/shard_map/ppermute | solution.py:27
  260.6 17.0 %collective-permute-start.3 = (bf16[324,512]{1,0:T(8,128)(2,1)S(1)}, bf16[324,512]{1,0:T(8,128)(2,1)S(1)}, u32[]{:S(2)}, u32[]{:S(2)}) collective-permute-start(bf16[324,512]{1,0:T(8,128)(2,1)S(1)} %get-tuple-element.14), channel_id=1, source_target_pairs={{0,128},{64,192},{128,0},{192,64},{1,129},{65,193},{129,1},{193,65... | collective-permute-start | bytes 995336 | tf_op jit(solution)/shard_map/ppermute | solution.py:27
  261.7 16.1 %collective-permute-start.2 = (bf16[324,512]{1,0:T(8,128)(2,1)S(1)}, bf16[324,512]{1,0:T(8,128)(2,1)S(1)}, u32[]{:S(2)}, u32[]{:S(2)}) collective-permute-start(bf16[324,512]{1,0:T(8,128)(2,1)S(1)} %get-tuple-element.15), channel_id=1, source_target_pairs={{0,64},{64,0},{128,192},{192,128},{1,65},{65,1},{129,193},{193,129... | collective-permute-start | bytes 995336 | tf_op jit(solution)/shard_map/ppermute | solution.py:27
